TPU v7x, 32 devices: a whole 2x2x4 slice. The times are simulated.
32 devices in a mesh: groups: 2 (over x), beam: 4 (over z), ctx: 4 (over y, core).
Axes of the slice: x: 2, y: 2, z: 4, core: 2. Of those that a mesh axis runs over, the one named last changes fastest.
Arguments:
- queries: bfloat16 [8, 16384], P(('groups', 'beam'), 'ctx'), parts along dimension 0
- new_keys: bfloat16 [8, 1024], P(('groups', 'beam')), parts along dimension 0, may hold values from -16 to 16
- new_values: bfloat16 [8, 1024], P(('groups', 'beam')), parts along dimension 0, may hold values from -9 to 9
- cache_keys: bfloat16 [8, 2048, 8, 128], P(('groups', 'beam'), 'ctx'), parts along dimension 0
- cache_values: bfloat16 [8, 2048, 8, 128], P(('groups', 'beam'), 'ctx'), parts along dimension 0, may hold values from -6 to 6
- parents: int32 [8], P('groups'), parts along dimension 0, may hold values from 0 to 3
- lengths: int32 [8], P('groups'), parts along dimension 0, may hold values from 8 to 16, as said below
- out_weight: bfloat16 [16384, 16384], P('ctx', 'beam'), may hold values from -0.046875 to 0.046875
Outputs:
- projected: bfloat16 [8, 16384], P('groups', ('beam', 'ctx')), parts along dimension 0
There are 2 independent parts, one for each index of `groups`. A program takes and returns all parts, laid end to end along the dimension named above; an argument that names none is the same for every part. Nothing has to cross between parts.
Inputs may be any that keep to these rules, and one draw needn't show every extreme that they name: `lengths`: each previous beam holds at least half of its 16 spans; in every draw some beam is full.
All inputs are finite; a program needn't handle non-finite values.
Results may differ from a plain program's by a relative error of at most 0.012.
Values may be sent and summed in bfloat16 or wider, within the bound.
No kernel may reach another device: no remote copies, remote signals or barrier semaphores. Data moves between devices by JAX's collectives and lax.ppermute only.
A program may use at most 64 MiB of HBM per device.

v0:
```python
import math

import jax
import jax.numpy as jnp
from jax import lax
from jax.experimental import pallas as pl
from jax.experimental.pallas import tpu as pltpu
from jax.sharding import PartitionSpec as P


H = 128
KVH = 8
HD = 128
SPAN = 128
GROUP = H // KVH

MASKED = -1e30
SCALE = 1.0 / math.sqrt(HD)

BF = jnp.bfloat16
F32 = jnp.float32
VMEM = pl.BlockSpec(memory_space=pltpu.VMEM)
HBM = pl.BlockSpec(memory_space=pltpu.HBM)
SHARES = (4, 5, 5, 5, 10, 3)


def params(mib):
    return pltpu.CompilerParams(vmem_limit_bytes=mib << 20)


def cost(flops, moved):
    return pl.CostEstimate(flops=flops, bytes_accessed=moved, transcendentals=0)


def partner(array, axis, k):
    return lax.ppermute(array, axis, [(i, i ^ k) for i in range(lax.axis_size(axis))])


def partners(arrays, axis):
    each = isinstance(arrays, (list, tuple))
    return [partner(arrays[k] if each else arrays, axis, k) for k in range(1, lax.axis_size(axis))]


def pack_kernel(heads, kv_count, q_hbm, k_hbm, v_hbm, out_ref, q_ref, k_ref, v_ref, rows, sems):
    copies = [
        pltpu.make_async_copy(src, dst, sems.at[n])
        for n, (src, dst) in enumerate(((q_hbm, q_ref), (k_hbm, k_ref), (v_hbm, v_ref)))
    ]
    for copy in copies:
        copy.start()
    start = lax.axis_index("ctx") * heads // GROUP
    rows[...] = jnp.zeros_like(rows)
    for copy in copies:
        copy.wait()
    for h in range(heads):
        rows[h : h + 1, :] = q_ref[:, h * HD : (h + 1) * HD].astype(F32)
    for r in range(kv_count):
        here = pl.ds(pl.multiple_of((start + r) * HD, HD), HD)
        rows[heads + r : heads + r + 1, :] = k_ref[:, here].astype(F32)
        rows[heads + kv_count + r : heads + kv_count + r + 1, :] = v_ref[:, here].astype(F32)
    out_ref[...] = rows[...].astype(BF)


def fetch_kernel(start, w_hbm, out_ref, sem):
    copy = pltpu.make_async_copy(w_hbm.at[pl.ds(start, out_ref.shape[0])], out_ref, sem)
    copy.start()
    copy.wait()


def relayout_kernel(start, k_hbm, v_hbm, w_hbm, kt, vt, piece, k_ref, v_ref, sems):
    copies = [
        pltpu.make_async_copy(src, dst, sems.at[n])
        for n, (src, dst) in enumerate(
            ((k_hbm, k_ref), (v_hbm, v_ref), (w_hbm.at[pl.ds(start, piece.shape[0])], piece))
        )
    ]
    for copy in copies:
        copy.start()
    copies[0].wait()
    kt[...] = pltpu.einshape("tkd->ktd", k_ref[0])
    copies[1].wait()
    vt[...] = pltpu.einshape("tkd->ktd", v_ref[0])
    copies[2].wait()


def stack_kernel(*refs):
    for n, ref in enumerate(refs[:-1]):
        refs[-1][n] = ref[...]


def split3(x):
    a = x.astype(BF)
    rest = x - a.astype(F32)
    b = rest.astype(BF)
    c = (rest - b.astype(F32)).astype(BF)
    return a, b, c


def eye(rows):
    shape = (rows, HD)
    return lax.broadcasted_iota(jnp.int32, shape, 0) == lax.broadcasted_iota(jnp.int32, shape, 1)


def attend_kernel(slots, start, beams, heads, kv_count, per_kv, tokens, *refs):
    n = len(slots)
    lengths_hbm, parents_hbm, w_hbm, kt, vt = refs[:5]
    stacks, outs = refs[5 : 5 + n], refs[5 + n : 5 + 2 * n]
    piece, lengths, parents, sems = refs[5 + 2 * n :]
    small = [
        pltpu.make_async_copy(lengths_hbm, lengths, sems.at[0]),
        pltpu.make_async_copy(parents_hbm, parents, sems.at[1]),
    ]
    large = pltpu.make_async_copy(w_hbm.at[pl.ds(start, piece.shape[0])], piece, sems.at[2])
    for copy in small:
        copy.start()
    large.start()
    b = lax.axis_index("beam")
    c = lax.axis_index("ctx")
    rows = beams * per_kv
    count = kv_count * rows
    pairs = [(i, r) for i in range(n) for r in range(kv_count)]

    def kv_head(i, r):
        return (c ^ slots[i]) * heads // GROUP + r

    scores = []
    for i, r in pairs:
        q = stacks[i][:, r * per_kv : (r + 1) * per_kv, :].astype(F32)
        q = q.reshape(rows, HD).astype(BF)
        scores.append(
            lax.dot_general(q, kt[kv_head(i, r)], (((1,), (1,)), ((), ())), preferred_element_type=F32)
        )
    for copy in small:
        copy.wait()
    limit = lengths[b] * SPAN - c * tokens
    keep = lax.broadcasted_iota(jnp.int32, (rows, tokens), 1) < limit
    scores = [jnp.where(keep, s * SCALE, MASKED) for s in scores]
    peaks = [jnp.max(s, axis=-1, keepdims=True) for s in scores]
    weights = [jnp.where(keep, jnp.exp(s - m), 0.0) for s, m in zip(scores, peaks)]
    totals = [jnp.sum(w, axis=-1, keepdims=True) for w in weights]
    blended = [
        jnp.dot(w.astype(BF), vt[kv_head(i, r)], preferred_element_type=F32)
        for w, (i, r) in zip(weights, pairs)
    ]
    safe = [jnp.where(t > 0.0, t, 1.0) for t in totals]
    lses = [jnp.where(t > 0.0, m + jnp.log(f), MASKED) for t, m, f in zip(totals, peaks, safe)]
    which = lax.broadcasted_iota(jnp.int32, (16, HD), 0)
    diagonal = eye(count)
    for i in range(n):
        mine = slice(i * kv_count, (i + 1) * kv_count)
        outs[i][0:count, :] = jnp.concatenate(
            [(o / f).astype(BF) for o, f in zip(blended[mine], safe[mine])], axis=0
        )
        lse = jnp.concatenate(lses[mine], axis=0)
        line = jnp.sum(jnp.where(diagonal, lse, 0.0), axis=0, keepdims=True)
        parts = [p.astype(F32) for p in split3(line)]
        stats = jnp.where(which == 0, parts[0], jnp.where(which == 1, parts[1], jnp.where(which == 2, parts[2], 0.0)))
        if slots[i] == 0:
            child = lax.broadcasted_iota(jnp.int32, (16, HD), 1) % rows // per_kv
            for k in range(beams):
                stats = jnp.where((which == 3) & (child == k) & (parents[b ^ k] == b), 1.0, stats)
        outs[i][count : count + 16, :] = stats.astype(BF)
    large.wait()


def merge_kernel(ctx_count, beams, heads, kv_count, per_kv, *refs):
    stack, states, out_ref = refs[0], refs[1 : 1 + ctx_count], refs[1 + ctx_count]
    b = lax.axis_index("beam")
    rows = beams * per_kv
    count = kv_count * rows
    diagonal = eye(count)
    own, value = [], []
    for r in range(kv_count):
        q = stack[:, r * per_kv : (r + 1) * per_kv, :].astype(F32)
        key = stack[:, heads + r : heads + r + 1, :].astype(F32)
        own.append(jnp.sum(q * key, axis=-1, keepdims=True).reshape(rows, 1) * SCALE)
        v = stack[:, heads + kv_count + r : heads + kv_count + r + 1, :].astype(F32)
        value.append(jnp.broadcast_to(v, (beams, per_kv, HD)).reshape(rows, HD))
    own = jnp.concatenate(own, axis=0) if kv_count > 1 else own[0]
    value = jnp.concatenate(value, axis=0) if kv_count > 1 else value[0]
    lses = []
    for k in range(ctx_count):
        line = states[k][count : count + 16, :].astype(F32)
        if k == 0:
            mine = jnp.sum(jnp.where(diagonal, line[3:4], 0.0), axis=-1, keepdims=True)
        line = line[0:1] + line[1:2] + line[2:3]
        lses.append(jnp.sum(jnp.where(diagonal, line, 0.0), axis=-1, keepdims=True))
    peak = own
    for lse in lses:
        peak = jnp.maximum(peak, lse)
    weight = jnp.exp(own - peak)
    total = weight
    blended = weight * value
    for k in range(ctx_count):
        weight = jnp.exp(lses[k] - peak)
        total = total + weight
        blended = blended + weight * states[k][0:count, :].astype(F32)
    result = jnp.where(mine > 0.0, blended / total, 0.0).astype(BF)
    for r in range(kv_count):
        for i in range(beams):
            at = r * rows + i * per_kv
            out_ref[b ^ i, r * per_kv : (r + 1) * per_kv, :] = result[at : at + per_kv, :]


def chunk(rows, pieces, bounds, beams, at, width):
    return sum(
        jnp.dot(rows[:, lo:hi], ref[:, pl.ds(at, width)], preferred_element_type=F32)
        for ref, lo, hi in zip(pieces, bounds, bounds[1:])
    )[:beams]


def project_kernel(ctx_count, far, beams, heads, bounds, *refs):
    held = len(bounds) - 2
    rows_of, pieces, w_hbm = refs[:beams], refs[beams : beams + held], refs[beams + held]
    outs, (last, wide), (laid, sem) = refs[beams + held + 1 : -4], refs[-4:-2], refs[-2:]
    copy = pltpu.make_async_copy(w_hbm.at[pl.ds(bounds[held], last.shape[0])], last, sem)
    copy.start()
    c = lax.axis_index("ctx")
    laid[...] = jnp.zeros_like(laid)
    for i in range(beams):
        row = rows_of[0][i].astype(F32)
        for k in range(1, beams):
            row = row + rows_of[k][i].astype(F32)
        laid[i * heads : (i + 1) * heads, :] = row
    for h in range(heads):
        wide[:, h * HD : (h + 1) * HD] = laid[pl.ds(h, 8, stride=heads), :].astype(BF)
    columns = last.shape[1] // ctx_count
    width = min(512, columns)
    places = [(n, k, j) for n, k in enumerate(far) for j in range(0, columns, width)]
    for n, k, j in places:
        at = pl.multiple_of((c ^ k) * columns + j, 128)
        outs[n][:, j : j + width] = chunk(wide, pieces, bounds[: held + 1], beams, at, width)
    copy.wait()
    for n, k, j in places:
        at = pl.multiple_of((c ^ k) * columns + j, 128)
        outs[n][:, j : j + width] += chunk(wide, [last], bounds[held:], beams, at, width)


def near_kernel(ctx_count, k, beams, bounds, wide, *refs):
    pieces, out_ref = refs[:-1], refs[-1]
    columns = pieces[0].shape[1] // ctx_count
    width = min(512, columns)
    for j in range(0, columns, width):
        at = pl.multiple_of((lax.axis_index("ctx") ^ k) * columns + j, 128)
        out_ref[:, j : j + width] = chunk(wide, pieces, bounds, beams, at, width)


def step(queries, new_keys, new_values, cache_keys, cache_values, parents, lengths, out_weight):
    ctx_count = lax.axis_size("ctx")
    beams = lax.axis_size("beam")
    heads = queries.shape[1] // HD
    tokens = cache_keys.shape[1]
    kv_count = max(1, heads // GROUP)
    per_kv = min(heads, GROUP)
    packet_rows = -(-(heads + 2 * kv_count) // 16) * 16
    count = beams * heads

    queries, new_keys, new_values, parents, lengths, out_weight = (
        pltpu.with_memory_space_constraint(x, pltpu.HBM)
        for x in (queries, new_keys, new_values, parents, lengths, out_weight)
    )
    cache_keys = pltpu.with_memory_space_constraint(cache_keys, pltpu.HBM)
    cache_values = pltpu.with_memory_space_constraint(cache_values, pltpu.HBM)
    bounds = [round(heads * sum(SHARES[:n]) / sum(SHARES)) * HD for n in range(len(SHARES) + 1)]
    piece = [jax.ShapeDtypeStruct((hi - lo, out_weight.shape[1]), BF) for lo, hi in zip(bounds, bounds[1:])]

    def fetch(n):
        return pl.pallas_call(
            lambda *refs: fetch_kernel(bounds[n], *refs),
            out_shape=piece[n],
            in_specs=[HBM],
            out_specs=VMEM,
            scratch_shapes=[pltpu.SemaphoreType.DMA],
            compiler_params=params(4),
            cost_estimate=cost(0, 2 * piece[n].size),
        )(out_weight)

    def attend(slots, n):
        return pl.pallas_call(
            lambda *refs: attend_kernel(slots, bounds[n], beams, heads, kv_count, per_kv, tokens, *refs),
            out_shape=[jax.ShapeDtypeStruct((count + 16, HD), BF)] * len(slots) + [piece[n]],
            in_specs=[HBM] * 3 + [VMEM] * (len(slots) + 2),
            out_specs=[VMEM] * (len(slots) + 1),
            scratch_shapes=[pltpu.SMEM(lengths.shape, jnp.int32)] * 2 + [pltpu.SemaphoreType.DMA((3,))],
            compiler_params=params(12),
            cost_estimate=cost(4 * count * len(slots) * tokens * HD, 2 * piece[n].size),
        )(lengths, parents, out_weight, kt, vt, *[stacks[k] for k in slots])

    packet = pl.pallas_call(
        lambda *refs: pack_kernel(heads, kv_count, *refs),
        out_shape=jax.ShapeDtypeStruct((packet_rows, HD), BF),
        in_specs=[HBM] * 3,
        out_specs=VMEM,
        scratch_shapes=[pltpu.VMEM(x.shape, BF) for x in (queries, new_keys, new_values)]
        + [pltpu.VMEM((packet_rows, HD), F32), pltpu.SemaphoreType.DMA((3,))],
        compiler_params=params(4),
        name="pack",
    )(queries, new_keys, new_values)
    turned = jax.ShapeDtypeStruct((KVH, tokens, HD), BF)
    kt, vt, piece0 = pl.pallas_call(
        lambda *refs: relayout_kernel(bounds[0], *refs),
        out_shape=[turned, turned, piece[0]],
        in_specs=[HBM] * 3,
        out_specs=[VMEM] * 3,
        scratch_shapes=[pltpu.VMEM(cache_keys.shape, BF)] * 2 + [pltpu.SemaphoreType.DMA((3,))],
        compiler_params=params(8),
        cost_estimate=cost(0, 4 * turned.size + 2 * piece[0].size),
        name="relayout",
    )(cache_keys, cache_values, out_weight)
    packets = [packet] + partners(packet, "beam")
    stack = pl.pallas_call(
        stack_kernel,
        out_shape=jax.ShapeDtypeStruct((beams,) + packet.shape, BF),
        in_specs=[VMEM] * beams,
        out_specs=VMEM,
        compiler_params=params(4),
        name="stack",
    )(*packets)
    stacks = [stack] + partners(stack, "ctx")
    own_state, piece1 = attend((0,), 1)
    *states, piece2 = attend(tuple(range(1, ctx_count)), 2)
    states = [own_state] + partners([None] + states, "ctx")
    piece3 = fetch(3)

    attended = pl.pallas_call(
        lambda *refs: merge_kernel(ctx_count, beams, heads, kv_count, per_kv, *refs),
        out_shape=jax.ShapeDtypeStruct((beams, heads, HD), BF),
        in_specs=[VMEM] * (1 + ctx_count),
        out_specs=VMEM,
        compiler_params=params(8),
        name="merge",
    )(stack, *states)
    rows_of = [attended] + partners(attended, "beam")

    piece4 = fetch(4)
    held = (piece0, piece1, piece2, piece3, piece4)

    columns = out_weight.shape[1] // ctx_count
    part = jax.ShapeDtypeStruct((beams, columns), F32)
    wide = jax.ShapeDtypeStruct((8, heads * HD), BF)
    far = tuple(range(2, ctx_count))
    *parts, piece5, wide = pl.pallas_call(
        lambda *refs: project_kernel(ctx_count, far, beams, heads, bounds, *refs),
        out_shape=[part] * len(far) + [piece[5], wide],
        in_specs=[VMEM] * (beams + len(held)) + [HBM],
        out_specs=[VMEM] * (len(far) + 2),
        scratch_shapes=[pltpu.VMEM((8 * heads, HD), F32), pltpu.SemaphoreType.DMA],
        compiler_params=params(8),
        cost_estimate=cost(8 * out_weight.size, 2 * piece[5].size),
        name="project",
    )(*rows_of, *held, out_weight)

    def near(k):
        return pl.pallas_call(
            lambda *refs: near_kernel(ctx_count, k, beams, bounds, *refs),
            out_shape=part,
            in_specs=[VMEM] * (len(held) + 2),
            out_specs=VMEM,
            compiler_params=params(4),
            cost_estimate=cost(4 * out_weight.size, 0),
        )(wide, *held, piece5)

    others = [partner(part, "ctx", k) for k, part in zip(far, parts)]
    core = near(1)
    others.append(partner(core, "ctx", 1))
    total = near(0)
    for other in others:
        total = total + other
    return total.astype(BF)


def solution(mesh):
    placed = (
        P(("groups", "beam"), "ctx"),
        P(("groups", "beam"), None),
        P(("groups", "beam"), None),
        P(("groups", "beam"), "ctx", None, None),
        P(("groups", "beam"), "ctx", None, None),
        P("groups"),
        P("groups"),
        P("ctx", "beam"),
    )
    return jax.shard_map(
        step,
        mesh=mesh,
        in_specs=placed,
        out_specs=P("groups", ("beam", "ctx")),
        check_vma=False,
    )
```

profile of v0, /device:TPU:0, one launch (start us, length us, event | category | flops | bytes accessed | tf_op | source)
XLA Modules:
  0.0 43.5 jit_solution(16202887684867022831)
XLA Ops:
  0.0 0.8 %pack.1.refs_0_ = bf16[48,128]{1,0:T(8,128)(2,1)S(1)} custom-call(bf16[1,4096]{1,0:T(2,128)(2,1)} %refs_0_.6, bf16[1,1024]{1,0:T(2,128)(2,1)} %refs_1_.4, bf16[1,1024]{1,0:T(2,128)(2,1)} %refs_2_.4), custom_call_target="tpu_custom_call" | custom-call | tf_op jit(solution)/shard_map/pack/pallas_call | solution.py:289
  0.8 5.1 %collective-permute-start.2 = (bf16[48,128]{1,0:T(8,128)(2,1)S(1)}, bf16[48,128]{1,0:T(8,128)(2,1)S(1)}, u32[]{:S(2)}, u32[]{:S(2)}) collective-permute-start(bf16[48,128]{1,0:T(8,128)(2,1)S(1)} %pack.1.refs_0_), channel_id=1, source_target_pairs={{0,12},{4,8},{8,4},{12,0},{1,13},{5,9},{9,5},{13,1},{2,14},{6,10},... | collective-permute-start | bytes 36872 | tf_op jit(solution)/shard_map/ppermute | solution.py:36
  5.9 0.6 %collective-permute-start = (bf16[48,128]{1,0:T(8,128)(2,1)S(1)}, bf16[48,128]{1,0:T(8,128)(2,1)S(1)}, u32[]{:S(2)}, u32[]{:S(2)}) collective-permute-start(bf16[48,128]{1,0:T(8,128)(2,1)S(1)} %pack.1.refs_0_), channel_id=1, source_target_pairs={{0,4},{4,0},{8,12},{12,8},{1,5},{5,1},{9,13},{13,9},{2,6},{6,2},{1... | collective-permute-start | bytes 36872 | tf_op jit(solution)/shard_map/ppermute | solution.py:36
  6.6 1.0 %collective-permute-done.2.refs_3_ = bf16[48,128]{1,0:T(8,128)(2,1)S(1)} collective-permute-done((bf16[48,128]{1,0:T(8,128)(2,1)S(1)}, bf16[48,128]{1,0:T(8,128)(2,1)S(1)}, u32[]{:S(2)}, u32[]{:S(2)}) %collective-permute-start.2) | collective-permute-done | bytes 12320 | tf_op jit(solution)/shard_map/ppermute | solution.py:36
  7.6 2.9 %collective-permute-done.1.refs_2_ = bf16[48,128]{1,0:T(8,128)(2,1)S(1)} collective-permute-done((bf16[48,128]{1,0:T(8,128)(2,1)S(1)}, bf16[48,128]{1,0:T(8,128)(2,1)S(1)}, u32[]{:S(2)}, u32[]{:S(2)}) %collective-permute-start.1) | collective-permute-done | bytes 12320 | tf_op jit(solution)/shard_map/ppermute | solution.py:36
  10.5 0.1 collective-permute-start.5
  10.6 1.6 %collective-permute-start.4 = (bf16[4,48,128]{2,1,0:T(8,128)(2,1)S(1)}, bf16[4,48,128]{2,1,0:T(8,128)(2,1)S(1)}, u32[]{:S(2)}, u32[]{:S(2)}) collective-permute-start(bf16[4,48,128]{2,1,0:T(8,128)(2,1)S(1)} %stack.1.refs_5_.refs_0_), channel_id=1, source_target_pairs={{0,2},{1,3},{2,0},{3,1},{4,6},{5,7},{6,4},{7,5},{8,10},{9,11},{10,... | collective-permute-start | bytes 147464 | tf_op jit(solution)/shard_map/ppermute | solution.py:36
  12.2 0.3 collective-permute-start.3
  12.5 2.9 %relayout.1 = (bf16[8,512,128]{2,1,0:T(8,128)(2,1)S(1)}, bf16[8,512,128]{2,1,0:T(8,128)(2,1)S(1)}, bf16[512,4096]{1,0:T(8,128)(2,1)S(1)}) custom-call(bf16[1,512,8,128]{3,2,1,0:T(8,128)(2,1)} %refs_0_.7, bf16[1,512,8,128]{3,2,1,0:T(8,128)(2,1)} %refs_1_.5, bf16[4096,4096]{1,0:T(8,128)(2,1)} %refs_9_.1), custom_call_target="tpu_custom_call" | custom-call | bytes 6291456 | tf_op jit(solution)/shard_map/relayout/pallas_call | solution.py:300
  15.3 0.0 collective-permute-done.5.refs_7_
  15.3 0.2 collective-permute-done.4.refs_6_
  15.5 0.0 collective-permute-done.3.refs_5_
  15.5 2.8 %shard_map.83 = (bf16[144,128]{1,0:T(8,128)(2,1)S(1)}, bf16[144,128]{1,0:T(8,128)(2,1)S(1)}, bf16[144,128]{1,0:T(8,128)(2,1)S(1)}, bf16[640,4096]{1,0:T(8,128)(2,1)S(1)}) custom-call(s32[4]{0:T(128)} %refs_0_.9, s32[4]{0:T(128)} %refs_1_.7, bf16[4096,4096]{1,0:T(8,128)(2,1)} %refs_9_.1, bf16[8,512,128]{2,1,0:T(8,128)(2,1)S(1)} %get-tuple-element.18.refs_3_, ...), custom_call_target="tpu_custom_call" | custom-call | flops 100663296 | bytes 5242880 | tf_op jit(solution)/shard_map/pallas_call | solution.py:279
  18.3 0.2 collective-permute-start.6
  18.5 1.4 %collective-permute-start.7 = (bf16[144,128]{1,0:T(8,128)(2,1)S(1)}, bf16[144,128]{1,0:T(8,128)(2,1)S(1)}, u32[]{:S(2)}, u32[]{:S(2)}) collective-permute-start(bf16[144,128]{1,0:T(8,128)(2,1)S(1)} %get-tuple-element.22), channel_id=1, source_target_pairs={{0,2},{1,3},{2,0},{3,1},{4,6},{5,7},{6,4},{7,5},{8,10},{9,11},{10,... | collective-permute-start | bytes 110600 | tf_op jit(solution)/shard_map/ppermute | solution.py:36
  19.8 0.4 collective-permute-start.8
  20.2 2.5 %shard_map.82 = (bf16[144,128]{1,0:T(8,128)(2,1)S(1)}, bf16[640,4096]{1,0:T(8,128)(2,1)S(1)}) custom-call(s32[4]{0:T(128)} %refs_0_.9, s32[4]{0:T(128)} %refs_1_.7, bf16[4096,4096]{1,0:T(8,128)(2,1)} %refs_9_.1, bf16[8,512,128]{2,1,0:T(8,128)(2,1)S(1)} %get-tuple-element.18.refs_3_, bf16[8,512,128]{2,1,0:T(8,128)(2,1)S(1)} %get-tuple-element.19.refs_4_, ...), custom_call_target="tpu_custom_call" | custom-call | flops 33554432 | bytes 5242880 | tf_op jit(solution)/shard_map/pallas_call | solution.py:279
  22.8 0.5 %collective-permute-done.8.refs_4_ = bf16[144,128]{1,0:T(8,128)(2,1)S(1)} collective-permute-done((bf16[144,128]{1,0:T(8,128)(2,1)S(1)}, bf16[144,128]{1,0:T(8,128)(2,1)S(1)}, u32[]{:S(2)}, u32[]{:S(2)}) %collective-permute-start.8) | collective-permute-done | bytes 36896 | tf_op jit(solution)/shard_map/ppermute | solution.py:36
  23.3 0.4 merge.1.refs_0_
  23.7 1.5 %collective-permute-start.11 = (bf16[4,32,128]{2,1,0:T(8,128)(2,1)S(1)}, bf16[4,32,128]{2,1,0:T(8,128)(2,1)S(1)}, u32[]{:S(2)}, u32[]{:S(2)}) collective-permute-start(bf16[4,32,128]{2,1,0:T(8,128)(2,1)S(1)} %merge.1.refs_0_), channel_id=1, source_target_pairs={{0,12},{4,8},{8,4},{12,0},{1,13},{5,9},{9,5},{13,1},{2,14},{6,10},... | collective-permute-start | bytes 98312 | tf_op jit(solution)/shard_map/ppermute | solution.py:36
  25.1 0.6 %collective-permute-start.10 = (bf16[4,32,128]{2,1,0:T(8,128)(2,1)S(1)}, bf16[4,32,128]{2,1,0:T(8,128)(2,1)S(1)}, u32[]{:S(2)}, u32[]{:S(2)}) collective-permute-start(bf16[4,32,128]{2,1,0:T(8,128)(2,1)S(1)} %merge.1.refs_0_), channel_id=1, source_target_pairs={{0,8},{4,12},{8,0},{12,4},{1,9},{5,13},{9,1},{13,5},{2,10},{6,14},... | collective-permute-start | bytes 98312 | tf_op jit(solution)/shard_map/ppermute | solution.py:36
  25.8 2.4 %collective-permute-start.9 = (bf16[4,32,128]{2,1,0:T(8,128)(2,1)S(1)}, bf16[4,32,128]{2,1,0:T(8,128)(2,1)S(1)}, u32[]{:S(2)}, u32[]{:S(2)}) collective-permute-start(bf16[4,32,128]{2,1,0:T(8,128)(2,1)S(1)} %merge.1.refs_0_), channel_id=1, source_target_pairs={{0,4},{4,0},{8,12},{12,8},{1,5},{5,1},{9,13},{13,9},{2,6},{6,2},{1... | collective-permute-start | bytes 98312 | tf_op jit(solution)/shard_map/ppermute | solution.py:36
  28.1 2.5 %shard_map.84.refs_7_.refs_4_ = bf16[640,4096]{1,0:T(8,128)(2,1)S(1)} custom-call(bf16[4096,4096]{1,0:T(8,128)(2,1)} %refs_9_.1), custom_call_target="tpu_custom_call" | custom-call | bytes 5242880 | tf_op jit(solution)/shard_map/pallas_call | solution.py:268
  30.6 4.0 %shard_map.85.refs_8_.refs_5_ = bf16[1280,4096]{1,0:T(8,128)(2,1)S(1)} custom-call(bf16[4096,4096]{1,0:T(8,128)(2,1)} %refs_9_.1), custom_call_target="tpu_custom_call" | custom-call | bytes 10485760 | tf_op jit(solution)/shard_map/pallas_call | solution.py:268
  34.7 2.9 %project.1 = (f32[4,1024]{1,0:T(4,128)S(1)}, f32[4,1024]{1,0:T(4,128)S(1)}, bf16[384,4096]{1,0:T(8,128)(2,1)S(1)}, bf16[8,4096]{1,0:T(8,128)(2,1)S(1)}) custom-call(bf16[4,32,128]{2,1,0:T(8,128)(2,1)S(1)} %merge.1.refs_0_, bf16[4,32,128]{2,1,0:T(8,128)(2,1)S(1)} %collective-permute-done.9.refs_1_, bf16[4,32,128]{2,1,0:T(8,128)(2,1)S(1)} %collective-permute-done.10.refs_2_, ...), custom_call_target="tpu_custom_call" | custom-call | flops 134217728 | bytes 3145728 | tf_op jit(solution)/shard_map/project/pallas_call | solution.py:342
  37.5 1.2 %shard_map.87 = f32[4,1024]{1,0:T(4,128)S(1)} custom-call(bf16[8,4096]{1,0:T(8,128)(2,1)S(1)} %get-tuple-element.27.refs_0_, bf16[512,4096]{1,0:T(8,128)(2,1)S(1)} %get-tuple-element.24.refs_4_.refs_1_, bf16[640,4096]{1,0:T(8,128)(2,1)S(1)} %get-tuple-element.25.refs_5_.refs_2_, bf16[640,4096]{1,0:T(8,128)(2,1)S(1)} %get-tuple-element.26.refs_6_.refs_3_, ...), custom_call_target="tpu_custom_call" | custom-call | flops 67108864 | tf_op jit(solution)/shard_map/pallas_call | solution.py:354
  38.7 1.0 %collective-permute-start.12 = (f32[4,1024]{1,0:T(4,128)S(1)}, f32[4,1024]{1,0:T(4,128)S(1)}, u32[]{:S(2)}, u32[]{:S(2)}) collective-permute-start(f32[4,1024]{1,0:T(4,128)S(1)} %get-tuple-element.29), channel_id=1, source_target_pairs={{0,2},{1,3},{2,0},{3,1},{4,6},{5,7},{6,4},{7,5},{8,10},{9,11},{10,... | collective-permute-start | bytes 49160 | tf_op jit(solution)/shard_map/ppermute | solution.py:36
  39.8 0.8 %collective-permute-start.13 = (f32[4,1024]{1,0:T(4,128)S(1)}, f32[4,1024]{1,0:T(4,128)S(1)}, u32[]{:S(2)}, u32[]{:S(2)}) collective-permute-start(f32[4,1024]{1,0:T(4,128)S(1)} %get-tuple-element.30), channel_id=1, source_target_pairs={{0,3},{1,2},{2,1},{3,0},{4,7},{5,6},{6,5},{7,4},{8,11},{9,10},{10,... | collective-permute-start | bytes 49160 | tf_op jit(solution)/shard_map/ppermute | solution.py:36
  40.6 1.2 %shard_map.86 = f32[4,1024]{1,0:T(4,128)S(1)} custom-call(bf16[8,4096]{1,0:T(8,128)(2,1)S(1)} %get-tuple-element.27.refs_0_, bf16[512,4096]{1,0:T(8,128)(2,1)S(1)} %get-tuple-element.24.refs_4_.refs_1_, bf16[640,4096]{1,0:T(8,128)(2,1)S(1)} %get-tuple-element.25.refs_5_.refs_2_, bf16[640,4096]{1,0:T(8,128)(2,1)S(1)} %get-tuple-element.26.refs_6_.refs_3_, ...), custom_call_target="tpu_custom_call" | custom-call | flops 67108864 | tf_op jit(solution)/shard_map/pallas_call | solution.py:354
  41.8 0.7 %collective-permute-done.12 = f32[4,1024]{1,0:T(4,128)S(1)} collective-permute-done((f32[4,1024]{1,0:T(4,128)S(1)}, f32[4,1024]{1,0:T(4,128)S(1)}, u32[]{:S(2)}, u32[]{:S(2)}) %collective-permute-start.12) | collective-permute-done | bytes 16416 | tf_op jit(solution)/shard_map/ppermute | solution.py:36
  42.5 0.4 collective-permute-done.13
  42.9 0.6 %add_convert_fusion = bf16[4,1024]{1,0:T(4,128)(2,1)} fusion(f32[4,1024]{1,0:T(4,128)S(1)} %collective-permute-done.14, f32[4,1024]{1,0:T(4,128)S(1)} %collective-permute-done.13, f32[4,1024]{1,0:T(4,128)S(1)} %shard_map.86, f32[4,1024]{1,0:T(4,128)S(1)} %collective-permute-done.12), kind=kLoop, calls=%fused_computation | loop fusion | flops 16384 | bytes 73728 | tf_op jit(solution)/shard_map/convert_element_type | solution.py:369
  (10 shorter events, 0.0 us)
Async XLA Ops:
  0.8 6.8 %collective-permute-start.2 = (bf16[48,128]{1,0:T(8,128)(2,1)S(1)}, bf16[48,128]{1,0:T(8,128)(2,1)S(1)}, u32[]{:S(2)}, u32[]{:S(2)}) collective-permute-start(bf16[48,128]{1,0:T(8,128)(2,1)S(1)} %pack.1.refs_0_), channel_id=1, source_target_pairs={{0,12},{4,8},{8,4},{12,0},{1,13},{5,9},{9,5},{13,1},{2,14},{6,10},... | collective-permute-start | bytes 36872 | tf_op jit(solution)/shard_map/ppermute | solution.py:36
  5.9 4.6 %collective-permute-start.1 = (bf16[48,128]{1,0:T(8,128)(2,1)S(1)}, bf16[48,128]{1,0:T(8,128)(2,1)S(1)}, u32[]{:S(2)}, u32[]{:S(2)}) collective-permute-start(bf16[48,128]{1,0:T(8,128)(2,1)S(1)} %pack.1.refs_0_), channel_id=1, source_target_pairs={{0,8},{4,12},{8,0},{12,4},{1,9},{5,13},{9,1},{13,5},{2,10},{6,14},... | collective-permute-start | bytes 36872 | tf_op jit(solution)/shard_map/ppermute | solution.py:36
  5.9 4.6 %collective-permute-start = (bf16[48,128]{1,0:T(8,128)(2,1)S(1)}, bf16[48,128]{1,0:T(8,128)(2,1)S(1)}, u32[]{:S(2)}, u32[]{:S(2)}) collective-permute-start(bf16[48,128]{1,0:T(8,128)(2,1)S(1)} %pack.1.refs_0_), channel_id=1, source_target_pairs={{0,4},{4,0},{8,12},{12,8},{1,5},{5,1},{9,13},{13,9},{2,6},{6,2},{1... | collective-permute-start | bytes 36872 | tf_op jit(solution)/shard_map/ppermute | solution.py:36
  10.5 4.8 %collective-permute-start.5 = (bf16[4,48,128]{2,1,0:T(8,128)(2,1)S(1)}, bf16[4,48,128]{2,1,0:T(8,128)(2,1)S(1)}, u32[]{:S(2)}, u32[]{:S(2)}) collective-permute-start(bf16[4,48,128]{2,1,0:T(8,128)(2,1)S(1)} %stack.1.refs_5_.refs_0_), channel_id=1, source_target_pairs={{0,3},{1,2},{2,1},{3,0},{4,7},{5,6},{6,5},{7,4},{8,11},{9,10},{10,... | collective-permute-start | bytes 147464 | tf_op jit(solution)/shard_map/ppermute | solution.py:36
  10.6 4.9 %collective-permute-start.4 = (bf16[4,48,128]{2,1,0:T(8,128)(2,1)S(1)}, bf16[4,48,128]{2,1,0:T(8,128)(2,1)S(1)}, u32[]{:S(2)}, u32[]{:S(2)}) collective-permute-start(bf16[4,48,128]{2,1,0:T(8,128)(2,1)S(1)} %stack.1.refs_5_.refs_0_), channel_id=1, source_target_pairs={{0,2},{1,3},{2,0},{3,1},{4,6},{5,7},{6,4},{7,5},{8,10},{9,11},{10,... | collective-permute-start | bytes 147464 | tf_op jit(solution)/shard_map/ppermute | solution.py:36
  12.2 3.3 %collective-permute-start.3 = (bf16[4,48,128]{2,1,0:T(8,128)(2,1)S(1)}, bf16[4,48,128]{2,1,0:T(8,128)(2,1)S(1)}, u32[]{:S(2)}, u32[]{:S(2)}) collective-permute-start(bf16[4,48,128]{2,1,0:T(8,128)(2,1)S(1)} %stack.1.refs_5_.refs_0_), channel_id=1, source_target_pairs={{0,1},{1,0},{2,3},{3,2},{4,5},{5,4},{6,7},{7,6},{8,9},{9,8},{10,11... | collective-permute-start | bytes 147464 | tf_op jit(solution)/shard_map/ppermute | solution.py:36
  18.3 4.5 %collective-permute-start.6 = (bf16[144,128]{1,0:T(8,128)(2,1)S(1)}, bf16[144,128]{1,0:T(8,128)(2,1)S(1)}, u32[]{:S(2)}, u32[]{:S(2)}) collective-permute-start(bf16[144,128]{1,0:T(8,128)(2,1)S(1)} %get-tuple-element.21), channel_id=1, source_target_pairs={{0,1},{1,0},{2,3},{3,2},{4,5},{5,4},{6,7},{7,6},{8,9},{9,8},{10,11... | collective-permute-start | bytes 110600 | tf_op jit(solution)/shard_map/ppermute | solution.py:36
  18.5 4.3 %collective-permute-start.7 = (bf16[144,128]{1,0:T(8,128)(2,1)S(1)}, bf16[144,128]{1,0:T(8,128)(2,1)S(1)}, u32[]{:S(2)}, u32[]{:S(2)}) collective-permute-start(bf16[144,128]{1,0:T(8,128)(2,1)S(1)} %get-tuple-element.22), channel_id=1, source_target_pairs={{0,2},{1,3},{2,0},{3,1},{4,6},{5,7},{6,4},{7,5},{8,10},{9,11},{10,... | collective-permute-start | bytes 110600 | tf_op jit(solution)/shard_map/ppermute | solution.py:36
  19.8 3.4 %collective-permute-start.8 = (bf16[144,128]{1,0:T(8,128)(2,1)S(1)}, bf16[144,128]{1,0:T(8,128)(2,1)S(1)}, u32[]{:S(2)}, u32[]{:S(2)}) collective-permute-start(bf16[144,128]{1,0:T(8,128)(2,1)S(1)} %get-tuple-element.23), channel_id=1, source_target_pairs={{0,3},{1,2},{2,1},{3,0},{4,7},{5,6},{6,5},{7,4},{8,11},{9,10},{10,... | collective-permute-start | bytes 110600 | tf_op jit(solution)/shard_map/ppermute | solution.py:36
  23.7 11.0 %collective-permute-start.11 = (bf16[4,32,128]{2,1,0:T(8,128)(2,1)S(1)}, bf16[4,32,128]{2,1,0:T(8,128)(2,1)S(1)}, u32[]{:S(2)}, u32[]{:S(2)}) collective-permute-start(bf16[4,32,128]{2,1,0:T(8,128)(2,1)S(1)} %merge.1.refs_0_), channel_id=1, source_target_pairs={{0,12},{4,8},{8,4},{12,0},{1,13},{5,9},{9,5},{13,1},{2,14},{6,10},... | collective-permute-start | bytes 98312 | tf_op jit(solution)/shard_map/ppermute | solution.py:36
  25.1 9.5 %collective-permute-start.10 = (bf16[4,32,128]{2,1,0:T(8,128)(2,1)S(1)}, bf16[4,32,128]{2,1,0:T(8,128)(2,1)S(1)}, u32[]{:S(2)}, u32[]{:S(2)}) collective-permute-start(bf16[4,32,128]{2,1,0:T(8,128)(2,1)S(1)} %merge.1.refs_0_), channel_id=1, source_target_pairs={{0,8},{4,12},{8,0},{12,4},{1,9},{5,13},{9,1},{13,5},{2,10},{6,14},... | collective-permute-start | bytes 98312 | tf_op jit(solution)/shard_map/ppermute | solution.py:36
  25.8 8.9 %collective-permute-start.9 = (bf16[4,32,128]{2,1,0:T(8,128)(2,1)S(1)}, bf16[4,32,128]{2,1,0:T(8,128)(2,1)S(1)}, u32[]{:S(2)}, u32[]{:S(2)}) collective-permute-start(bf16[4,32,128]{2,1,0:T(8,128)(2,1)S(1)} %merge.1.refs_0_), channel_id=1, source_target_pairs={{0,4},{4,0},{8,12},{12,8},{1,5},{5,1},{9,13},{13,9},{2,6},{6,2},{1... | collective-permute-start | bytes 98312 | tf_op jit(solution)/shard_map/ppermute | solution.py:36
  38.7 3.1 %collective-permute-start.14 = (f32[4,1024]{1,0:T(4,128)S(1)}, f32[4,1024]{1,0:T(4,128)S(1)}, u32[]{:S(2)}, u32[]{:S(2)}) collective-permute-start(f32[4,1024]{1,0:T(4,128)S(1)} %shard_map.87), channel_id=1, source_target_pairs={{0,1},{1,0},{2,3},{3,2},{4,5},{5,4},{6,7},{7,6},{8,9},{9,8},{10,11... | collective-permute-start | bytes 49160 | tf_op jit(solution)/shard_map/ppermute | solution.py:36
  38.7 3.8 %collective-permute-start.12 = (f32[4,1024]{1,0:T(4,128)S(1)}, f32[4,1024]{1,0:T(4,128)S(1)}, u32[]{:S(2)}, u32[]{:S(2)}) collective-permute-start(f32[4,1024]{1,0:T(4,128)S(1)} %get-tuple-element.29), channel_id=1, source_target_pairs={{0,2},{1,3},{2,0},{3,1},{4,6},{5,7},{6,4},{7,5},{8,10},{9,11},{10,... | collective-permute-start | bytes 49160 | tf_op jit(solution)/shard_map/ppermute | solution.py:36
  39.8 3.2 %collective-permute-start.13 = (f32[4,1024]{1,0:T(4,128)S(1)}, f32[4,1024]{1,0:T(4,128)S(1)}, u32[]{:S(2)}, u32[]{:S(2)}) collective-permute-start(f32[4,1024]{1,0:T(4,128)S(1)} %get-tuple-element.30), channel_id=1, source_target_pairs={{0,3},{1,2},{2,1},{3,0},{4,7},{5,6},{6,5},{7,4},{8,11},{9,10},{10,... | collective-permute-start | bytes 49160 | tf_op jit(solution)/shard_map/ppermute | solution.py:36
where the time goes:
time: 43.9 us; the launch traced here: 43.5 us
  Pallas kernels  21.1 us (48%)
  starting transfers between devices  16 us (36%)
  waiting for transfers between devices  5.76 us (13%)
  other arithmetic  0.61 us (1%)
    ppermute x15, starting transfers between devices, partner(): lax.ppermute(array, axis, [(i, i ^ k) for i in range(lax.axis_size(axis))])  16 us
    pallas_call x2, Pallas kernels, fetch(): pl.pallas_call(lambda *refs: fetch_kernel(bounds[n], *refs), out_shape=pi...  6.48 us
    ppermute x15, waiting for transfers between devices, partner(): lax.ppermute(array, axis, [(i, i ^ k) for i in range(lax.axis_size(axis))])  5.76 us
    pallas_call x2, Pallas kernels, attend(): pl.pallas_call(lambda *refs: attend_kernel(slots, bounds[n], beams, heads...  5.32 us
    pallas_call x1, Pallas kernels, step(): pl.pallas_call(lambda *refs: project_kernel(ctx_count, far, beams, heads,...  2.87 us
    pallas_call x1, Pallas kernels, step(): pl.pallas_call(lambda *refs: relayout_kernel(bounds[0], *refs), out_shape...  2.86 us
    pallas_call x2, Pallas kernels, near(): pl.pallas_call(lambda *refs: near_kernel(ctx_count, k, beams, bounds, *re...  2.38 us
  transfers between devices with their start and end apart: 15, of which 6 were waited for; matrix products, arithmetic and copies ran while one was open for 0% of the time, Pallas kernels for 30%

commit v1 on v0

--- a/solution.py
+++ b/solution.py
@@ -21,7 +21,7 @@
 F32 = jnp.float32
 VMEM = pl.BlockSpec(memory_space=pltpu.VMEM)
 HBM = pl.BlockSpec(memory_space=pltpu.HBM)
-SHARES = (4, 5, 5, 5, 10, 3)
+SHARES = (4, 5, 5, 6, 10, 2)
 
 
 def params(mib):
@@ -261,7 +261,8 @@
     )
     cache_keys = pltpu.with_memory_space_constraint(cache_keys, pltpu.HBM)
     cache_values = pltpu.with_memory_space_constraint(cache_values, pltpu.HBM)
-    bounds = [round(heads * sum(SHARES[:n]) / sum(SHARES)) * HD for n in range(len(SHARES) + 1)]
+    ends = [round(heads * sum(SHARES[:n]) / sum(SHARES)) for n in range(len(SHARES) + 1)]
+    bounds = [min(end, heads - len(SHARES) + n) * HD for n, end in enumerate(ends)]
     piece = [jax.ShapeDtypeStruct((hi - lo, out_weight.shape[1]), BF) for lo, hi in zip(bounds, bounds[1:])]
 
     def fetch(n):

time: 43.9 us -> 43.8 us (level)
  transfers between devices with their start and end apart: 15 -> 15, of which waited for: 6 -> 6; matrix products, arithmetic and copies ran while one was open for 0% -> 0% of each run, Pallas kernels for 30% -> 31%
where the time goes in v1:
time: 43.8 us; the launch traced here: 43.5 us
  Pallas kernels  21.1 us (48%)
  starting transfers between devices  16 us (37%)
  waiting for transfers between devices  5.76 us (13%)
  other arithmetic  0.61 us (1%)
    ppermute x15, starting transfers between devices, partner(): lax.ppermute(array, axis, [(i, i ^ k) for i in range(lax.axis_size(axis))])  16 us
    pallas_call x2, Pallas kernels, fetch(): pl.pallas_call(lambda *refs: fetch_kernel(bounds[n], *refs), out_shape=pi...  6.8 us
    ppermute x15, waiting for transfers between devices, partner(): lax.ppermute(array, axis, [(i, i ^ k) for i in range(lax.axis_size(axis))])  5.76 us
    pallas_call x2, Pallas kernels, attend(): pl.pallas_call(lambda *refs: attend_kernel(slots, bounds[n], beams, heads...  5.32 us
    pallas_call x1, Pallas kernels, step(): pl.pallas_call(lambda *refs: relayout_kernel(bounds[0], *refs), out_shape...  2.86 us
    pallas_call x1, Pallas kernels, step(): pl.pallas_call(lambda *refs: project_kernel(ctx_count, far, beams, heads,...  2.52 us
    pallas_call x2, Pallas kernels, near(): pl.pallas_call(lambda *refs: near_kernel(ctx_count, k, beams, bounds, *re...  2.38 us
  transfers between devices with their start and end apart: 15, of which 6 were waited for; matrix products, arithmetic and copies ran while one was open for 0% of the time, Pallas kernels for 31%

profile of v1, /device:TPU:0, one launch (start us, length us, event | category | flops | bytes accessed | tf_op | source)
XLA Modules:
  0.0 43.5 jit_solution(13293125816766443020)
XLA Ops:
  0.0 0.8 %pack.1.refs_0_ = bf16[48,128]{1,0:T(8,128)(2,1)S(1)} custom-call(bf16[1,4096]{1,0:T(2,128)(2,1)} %refs_0_.6, bf16[1,1024]{1,0:T(2,128)(2,1)} %refs_1_.4, bf16[1,1024]{1,0:T(2,128)(2,1)} %refs_2_.4), custom_call_target="tpu_custom_call" | custom-call | tf_op jit(solution)/shard_map/pack/pallas_call | solution.py:290
  0.8 5.1 %collective-permute-start.2 = (bf16[48,128]{1,0:T(8,128)(2,1)S(1)}, bf16[48,128]{1,0:T(8,128)(2,1)S(1)}, u32[]{:S(2)}, u32[]{:S(2)}) collective-permute-start(bf16[48,128]{1,0:T(8,128)(2,1)S(1)} %pack.1.refs_0_), channel_id=1, source_target_pairs={{0,12},{4,8},{8,4},{12,0},{1,13},{5,9},{9,5},{13,1},{2,14},{6,10},... | collective-permute-start | bytes 36872 | tf_op jit(solution)/shard_map/ppermute | solution.py:36
  5.9 0.6 %collective-permute-start = (bf16[48,128]{1,0:T(8,128)(2,1)S(1)}, bf16[48,128]{1,0:T(8,128)(2,1)S(1)}, u32[]{:S(2)}, u32[]{:S(2)}) collective-permute-start(bf16[48,128]{1,0:T(8,128)(2,1)S(1)} %pack.1.refs_0_), channel_id=1, source_target_pairs={{0,4},{4,0},{8,12},{12,8},{1,5},{5,1},{9,13},{13,9},{2,6},{6,2},{1... | collective-permute-start | bytes 36872 | tf_op jit(solution)/shard_map/ppermute | solution.py:36
  6.6 1.0 %collective-permute-done.2.refs_3_ = bf16[48,128]{1,0:T(8,128)(2,1)S(1)} collective-permute-done((bf16[48,128]{1,0:T(8,128)(2,1)S(1)}, bf16[48,128]{1,0:T(8,128)(2,1)S(1)}, u32[]{:S(2)}, u32[]{:S(2)}) %collective-permute-start.2) | collective-permute-done | bytes 12320 | tf_op jit(solution)/shard_map/ppermute | solution.py:36
  7.6 2.9 %collective-permute-done.1.refs_2_ = bf16[48,128]{1,0:T(8,128)(2,1)S(1)} collective-permute-done((bf16[48,128]{1,0:T(8,128)(2,1)S(1)}, bf16[48,128]{1,0:T(8,128)(2,1)S(1)}, u32[]{:S(2)}, u32[]{:S(2)}) %collective-permute-start.1) | collective-permute-done | bytes 12320 | tf_op jit(solution)/shard_map/ppermute | solution.py:36
  10.5 0.1 collective-permute-start.5
  10.6 1.6 %collective-permute-start.4 = (bf16[4,48,128]{2,1,0:T(8,128)(2,1)S(1)}, bf16[4,48,128]{2,1,0:T(8,128)(2,1)S(1)}, u32[]{:S(2)}, u32[]{:S(2)}) collective-permute-start(bf16[4,48,128]{2,1,0:T(8,128)(2,1)S(1)} %stack.1.refs_5_.refs_0_), channel_id=1, source_target_pairs={{0,2},{1,3},{2,0},{3,1},{4,6},{5,7},{6,4},{7,5},{8,10},{9,11},{10,... | collective-permute-start | bytes 147464 | tf_op jit(solution)/shard_map/ppermute | solution.py:36
  12.2 0.3 collective-permute-start.3
  12.5 2.9 %relayout.1 = (bf16[8,512,128]{2,1,0:T(8,128)(2,1)S(1)}, bf16[8,512,128]{2,1,0:T(8,128)(2,1)S(1)}, bf16[512,4096]{1,0:T(8,128)(2,1)S(1)}) custom-call(bf16[1,512,8,128]{3,2,1,0:T(8,128)(2,1)} %refs_0_.7, bf16[1,512,8,128]{3,2,1,0:T(8,128)(2,1)} %refs_1_.5, bf16[4096,4096]{1,0:T(8,128)(2,1)} %refs_9_.1), custom_call_target="tpu_custom_call" | custom-call | bytes 6291456 | tf_op jit(solution)/shard_map/relayout/pallas_call | solution.py:301
  15.3 0.0 collective-permute-done.5.refs_7_
  15.3 0.2 collective-permute-done.4.refs_6_
  15.5 0.0 collective-permute-done.3.refs_5_
  15.5 2.8 %shard_map.83 = (bf16[144,128]{1,0:T(8,128)(2,1)S(1)}, bf16[144,128]{1,0:T(8,128)(2,1)S(1)}, bf16[144,128]{1,0:T(8,128)(2,1)S(1)}, bf16[640,4096]{1,0:T(8,128)(2,1)S(1)}) custom-call(s32[4]{0:T(128)} %refs_0_.9, s32[4]{0:T(128)} %refs_1_.7, bf16[4096,4096]{1,0:T(8,128)(2,1)} %refs_9_.1, bf16[8,512,128]{2,1,0:T(8,128)(2,1)S(1)} %get-tuple-element.18.refs_3_, ...), custom_call_target="tpu_custom_call" | custom-call | flops 100663296 | bytes 5242880 | tf_op jit(solution)/shard_map/pallas_call | solution.py:280
  18.3 0.2 collective-permute-start.6
  18.5 1.4 %collective-permute-start.7 = (bf16[144,128]{1,0:T(8,128)(2,1)S(1)}, bf16[144,128]{1,0:T(8,128)(2,1)S(1)}, u32[]{:S(2)}, u32[]{:S(2)}) collective-permute-start(bf16[144,128]{1,0:T(8,128)(2,1)S(1)} %get-tuple-element.22), channel_id=1, source_target_pairs={{0,2},{1,3},{2,0},{3,1},{4,6},{5,7},{6,4},{7,5},{8,10},{9,11},{10,... | collective-permute-start | bytes 110600 | tf_op jit(solution)/shard_map/ppermute | solution.py:36
  19.8 0.4 collective-permute-start.8
  20.2 2.5 %shard_map.82 = (bf16[144,128]{1,0:T(8,128)(2,1)S(1)}, bf16[640,4096]{1,0:T(8,128)(2,1)S(1)}) custom-call(s32[4]{0:T(128)} %refs_0_.9, s32[4]{0:T(128)} %refs_1_.7, bf16[4096,4096]{1,0:T(8,128)(2,1)} %refs_9_.1, bf16[8,512,128]{2,1,0:T(8,128)(2,1)S(1)} %get-tuple-element.18.refs_3_, bf16[8,512,128]{2,1,0:T(8,128)(2,1)S(1)} %get-tuple-element.19.refs_4_, ...), custom_call_target="tpu_custom_call" | custom-call | flops 33554432 | bytes 5242880 | tf_op jit(solution)/shard_map/pallas_call | solution.py:280
  22.8 0.5 %collective-permute-done.8.refs_4_ = bf16[144,128]{1,0:T(8,128)(2,1)S(1)} collective-permute-done((bf16[144,128]{1,0:T(8,128)(2,1)S(1)}, bf16[144,128]{1,0:T(8,128)(2,1)S(1)}, u32[]{:S(2)}, u32[]{:S(2)}) %collective-permute-start.8) | collective-permute-done | bytes 36896 | tf_op jit(solution)/shard_map/ppermute | solution.py:36
  23.3 0.4 merge.1.refs_0_
  23.7 1.5 %collective-permute-start.11 = (bf16[4,32,128]{2,1,0:T(8,128)(2,1)S(1)}, bf16[4,32,128]{2,1,0:T(8,128)(2,1)S(1)}, u32[]{:S(2)}, u32[]{:S(2)}) collective-permute-start(bf16[4,32,128]{2,1,0:T(8,128)(2,1)S(1)} %merge.1.refs_0_), channel_id=1, source_target_pairs={{0,12},{4,8},{8,4},{12,0},{1,13},{5,9},{9,5},{13,1},{2,14},{6,10},... | collective-permute-start | bytes 98312 | tf_op jit(solution)/shard_map/ppermute | solution.py:36
  25.1 0.6 %collective-permute-start.10 = (bf16[4,32,128]{2,1,0:T(8,128)(2,1)S(1)}, bf16[4,32,128]{2,1,0:T(8,128)(2,1)S(1)}, u32[]{:S(2)}, u32[]{:S(2)}) collective-permute-start(bf16[4,32,128]{2,1,0:T(8,128)(2,1)S(1)} %merge.1.refs_0_), channel_id=1, source_target_pairs={{0,8},{4,12},{8,0},{12,4},{1,9},{5,13},{9,1},{13,5},{2,10},{6,14},... | collective-permute-start | bytes 98312 | tf_op jit(solution)/shard_map/ppermute | solution.py:36
  25.8 2.4 %collective-permute-start.9 = (bf16[4,32,128]{2,1,0:T(8,128)(2,1)S(1)}, bf16[4,32,128]{2,1,0:T(8,128)(2,1)S(1)}, u32[]{:S(2)}, u32[]{:S(2)}) collective-permute-start(bf16[4,32,128]{2,1,0:T(8,128)(2,1)S(1)} %merge.1.refs_0_), channel_id=1, source_target_pairs={{0,4},{4,0},{8,12},{12,8},{1,5},{5,1},{9,13},{13,9},{2,6},{6,2},{1... | collective-permute-start | bytes 98312 | tf_op jit(solution)/shard_map/ppermute | solution.py:36
  28.1 2.8 %shard_map.84.refs_7_.refs_4_ = bf16[768,4096]{1,0:T(8,128)(2,1)S(1)} custom-call(bf16[4096,4096]{1,0:T(8,128)(2,1)} %refs_9_.1), custom_call_target="tpu_custom_call" | custom-call | bytes 6291456 | tf_op jit(solution)/shard_map/pallas_call | solution.py:269
  30.9 4.0 %shard_map.85.refs_8_.refs_5_ = bf16[1280,4096]{1,0:T(8,128)(2,1)S(1)} custom-call(bf16[4096,4096]{1,0:T(8,128)(2,1)} %refs_9_.1), custom_call_target="tpu_custom_call" | custom-call | bytes 10485760 | tf_op jit(solution)/shard_map/pallas_call | solution.py:269
  35.0 2.5 %project.1 = (f32[4,1024]{1,0:T(4,128)S(1)}, f32[4,1024]{1,0:T(4,128)S(1)}, bf16[256,4096]{1,0:T(8,128)(2,1)S(1)}, bf16[8,4096]{1,0:T(8,128)(2,1)S(1)}) custom-call(bf16[4,32,128]{2,1,0:T(8,128)(2,1)S(1)} %merge.1.refs_0_, bf16[4,32,128]{2,1,0:T(8,128)(2,1)S(1)} %collective-permute-done.9.refs_1_, bf16[4,32,128]{2,1,0:T(8,128)(2,1)S(1)} %collective-permute-done.10.refs_2_, ...), custom_call_target="tpu_custom_call" | custom-call | flops 134217728 | bytes 2097152 | tf_op jit(solution)/shard_map/project/pallas_call | solution.py:343
  37.5 1.2 %shard_map.87 = f32[4,1024]{1,0:T(4,128)S(1)} custom-call(bf16[8,4096]{1,0:T(8,128)(2,1)S(1)} %get-tuple-element.27.refs_0_, bf16[512,4096]{1,0:T(8,128)(2,1)S(1)} %get-tuple-element.24.refs_4_.refs_1_, bf16[640,4096]{1,0:T(8,128)(2,1)S(1)} %get-tuple-element.25.refs_5_.refs_2_, bf16[640,4096]{1,0:T(8,128)(2,1)S(1)} %get-tuple-element.26.refs_6_.refs_3_, ...), custom_call_target="tpu_custom_call" | custom-call | flops 67108864 | tf_op jit(solution)/shard_map/pallas_call | solution.py:355
  38.7 1.0 %collective-permute-start.12 = (f32[4,1024]{1,0:T(4,128)S(1)}, f32[4,1024]{1,0:T(4,128)S(1)}, u32[]{:S(2)}, u32[]{:S(2)}) collective-permute-start(f32[4,1024]{1,0:T(4,128)S(1)} %get-tuple-element.29), channel_id=1, source_target_pairs={{0,2},{1,3},{2,0},{3,1},{4,6},{5,7},{6,4},{7,5},{8,10},{9,11},{10,... | collective-permute-start | bytes 49160 | tf_op jit(solution)/shard_map/ppermute | solution.py:36
  39.7 0.8 %collective-permute-start.13 = (f32[4,1024]{1,0:T(4,128)S(1)}, f32[4,1024]{1,0:T(4,128)S(1)}, u32[]{:S(2)}, u32[]{:S(2)}) collective-permute-start(f32[4,1024]{1,0:T(4,128)S(1)} %get-tuple-element.30), channel_id=1, source_target_pairs={{0,3},{1,2},{2,1},{3,0},{4,7},{5,6},{6,5},{7,4},{8,11},{9,10},{10,... | collective-permute-start | bytes 49160 | tf_op jit(solution)/shard_map/ppermute | solution.py:36
  40.6 1.2 %shard_map.86 = f32[4,1024]{1,0:T(4,128)S(1)} custom-call(bf16[8,4096]{1,0:T(8,128)(2,1)S(1)} %get-tuple-element.27.refs_0_, bf16[512,4096]{1,0:T(8,128)(2,1)S(1)} %get-tuple-element.24.refs_4_.refs_1_, bf16[640,4096]{1,0:T(8,128)(2,1)S(1)} %get-tuple-element.25.refs_5_.refs_2_, bf16[640,4096]{1,0:T(8,128)(2,1)S(1)} %get-tuple-element.26.refs_6_.refs_3_, ...), custom_call_target="tpu_custom_call" | custom-call | flops 67108864 | tf_op jit(solution)/shard_map/pallas_call | solution.py:355
  41.8 0.7 %collective-permute-done.12 = f32[4,1024]{1,0:T(4,128)S(1)} collective-permute-done((f32[4,1024]{1,0:T(4,128)S(1)}, f32[4,1024]{1,0:T(4,128)S(1)}, u32[]{:S(2)}, u32[]{:S(2)}) %collective-permute-start.12) | collective-permute-done | bytes 16416 | tf_op jit(solution)/shard_map/ppermute | solution.py:36
  42.5 0.4 collective-permute-done.13
  42.9 0.6 %add_convert_fusion = bf16[4,1024]{1,0:T(4,128)(2,1)} fusion(f32[4,1024]{1,0:T(4,128)S(1)} %collective-permute-done.14, f32[4,1024]{1,0:T(4,128)S(1)} %collective-permute-done.13, f32[4,1024]{1,0:T(4,128)S(1)} %shard_map.86, f32[4,1024]{1,0:T(4,128)S(1)} %collective-permute-done.12), kind=kLoop, calls=%fused_computation | loop fusion | flops 16384 | bytes 73728 | tf_op jit(solution)/shard_map/convert_element_type | solution.py:370
  (10 shorter events, 0.0 us)
Async XLA Ops:
  0.8 6.8 %collective-permute-start.2 = (bf16[48,128]{1,0:T(8,128)(2,1)S(1)}, bf16[48,128]{1,0:T(8,128)(2,1)S(1)}, u32[]{:S(2)}, u32[]{:S(2)}) collective-permute-start(bf16[48,128]{1,0:T(8,128)(2,1)S(1)} %pack.1.refs_0_), channel_id=1, source_target_pairs={{0,12},{4,8},{8,4},{12,0},{1,13},{5,9},{9,5},{13,1},{2,14},{6,10},... | collective-permute-start | bytes 36872 | tf_op jit(solution)/shard_map/ppermute | solution.py:36
  5.9 4.6 %collective-permute-start.1 = (bf16[48,128]{1,0:T(8,128)(2,1)S(1)}, bf16[48,128]{1,0:T(8,128)(2,1)S(1)}, u32[]{:S(2)}, u32[]{:S(2)}) collective-permute-start(bf16[48,128]{1,0:T(8,128)(2,1)S(1)} %pack.1.refs_0_), channel_id=1, source_target_pairs={{0,8},{4,12},{8,0},{12,4},{1,9},{5,13},{9,1},{13,5},{2,10},{6,14},... | collective-permute-start | bytes 36872 | tf_op jit(solution)/shard_map/ppermute | solution.py:36
  5.9 4.6 %collective-permute-start = (bf16[48,128]{1,0:T(8,128)(2,1)S(1)}, bf16[48,128]{1,0:T(8,128)(2,1)S(1)}, u32[]{:S(2)}, u32[]{:S(2)}) collective-permute-start(bf16[48,128]{1,0:T(8,128)(2,1)S(1)} %pack.1.refs_0_), channel_id=1, source_target_pairs={{0,4},{4,0},{8,12},{12,8},{1,5},{5,1},{9,13},{13,9},{2,6},{6,2},{1... | collective-permute-start | bytes 36872 | tf_op jit(solution)/shard_map/ppermute | solution.py:36
  10.5 4.8 %collective-permute-start.5 = (bf16[4,48,128]{2,1,0:T(8,128)(2,1)S(1)}, bf16[4,48,128]{2,1,0:T(8,128)(2,1)S(1)}, u32[]{:S(2)}, u32[]{:S(2)}) collective-permute-start(bf16[4,48,128]{2,1,0:T(8,128)(2,1)S(1)} %stack.1.refs_5_.refs_0_), channel_id=1, source_target_pairs={{0,3},{1,2},{2,1},{3,0},{4,7},{5,6},{6,5},{7,4},{8,11},{9,10},{10,... | collective-permute-start | bytes 147464 | tf_op jit(solution)/shard_map/ppermute | solution.py:36
  10.6 4.9 %collective-permute-start.4 = (bf16[4,48,128]{2,1,0:T(8,128)(2,1)S(1)}, bf16[4,48,128]{2,1,0:T(8,128)(2,1)S(1)}, u32[]{:S(2)}, u32[]{:S(2)}) collective-permute-start(bf16[4,48,128]{2,1,0:T(8,128)(2,1)S(1)} %stack.1.refs_5_.refs_0_), channel_id=1, source_target_pairs={{0,2},{1,3},{2,0},{3,1},{4,6},{5,7},{6,4},{7,5},{8,10},{9,11},{10,... | collective-permute-start | bytes 147464 | tf_op jit(solution)/shard_map/ppermute | solution.py:36
  12.2 3.3 %collective-permute-start.3 = (bf16[4,48,128]{2,1,0:T(8,128)(2,1)S(1)}, bf16[4,48,128]{2,1,0:T(8,128)(2,1)S(1)}, u32[]{:S(2)}, u32[]{:S(2)}) collective-permute-start(bf16[4,48,128]{2,1,0:T(8,128)(2,1)S(1)} %stack.1.refs_5_.refs_0_), channel_id=1, source_target_pairs={{0,1},{1,0},{2,3},{3,2},{4,5},{5,4},{6,7},{7,6},{8,9},{9,8},{10,11... | collective-permute-start | bytes 147464 | tf_op jit(solution)/shard_map/ppermute | solution.py:36
  18.3 4.5 %collective-permute-start.6 = (bf16[144,128]{1,0:T(8,128)(2,1)S(1)}, bf16[144,128]{1,0:T(8,128)(2,1)S(1)}, u32[]{:S(2)}, u32[]{:S(2)}) collective-permute-start(bf16[144,128]{1,0:T(8,128)(2,1)S(1)} %get-tuple-element.21), channel_id=1, source_target_pairs={{0,1},{1,0},{2,3},{3,2},{4,5},{5,4},{6,7},{7,6},{8,9},{9,8},{10,11... | collective-permute-start | bytes 110600 | tf_op jit(solution)/shard_map/ppermute | solution.py:36
  18.5 4.3 %collective-permute-start.7 = (bf16[144,128]{1,0:T(8,128)(2,1)S(1)}, bf16[144,128]{1,0:T(8,128)(2,1)S(1)}, u32[]{:S(2)}, u32[]{:S(2)}) collective-permute-start(bf16[144,128]{1,0:T(8,128)(2,1)S(1)} %get-tuple-element.22), channel_id=1, source_target_pairs={{0,2},{1,3},{2,0},{3,1},{4,6},{5,7},{6,4},{7,5},{8,10},{9,11},{10,... | collective-permute-start | bytes 110600 | tf_op jit(solution)/shard_map/ppermute | solution.py:36
  19.8 3.4 %collective-permute-start.8 = (bf16[144,128]{1,0:T(8,128)(2,1)S(1)}, bf16[144,128]{1,0:T(8,128)(2,1)S(1)}, u32[]{:S(2)}, u32[]{:S(2)}) collective-permute-start(bf16[144,128]{1,0:T(8,128)(2,1)S(1)} %get-tuple-element.23), channel_id=1, source_target_pairs={{0,3},{1,2},{2,1},{3,0},{4,7},{5,6},{6,5},{7,4},{8,11},{9,10},{10,... | collective-permute-start | bytes 110600 | tf_op jit(solution)/shard_map/ppermute | solution.py:36
  23.7 11.3 %collective-permute-start.11 = (bf16[4,32,128]{2,1,0:T(8,128)(2,1)S(1)}, bf16[4,32,128]{2,1,0:T(8,128)(2,1)S(1)}, u32[]{:S(2)}, u32[]{:S(2)}) collective-permute-start(bf16[4,32,128]{2,1,0:T(8,128)(2,1)S(1)} %merge.1.refs_0_), channel_id=1, source_target_pairs={{0,12},{4,8},{8,4},{12,0},{1,13},{5,9},{9,5},{13,1},{2,14},{6,10},... | collective-permute-start | bytes 98312 | tf_op jit(solution)/shard_map/ppermute | solution.py:36
  25.1 9.8 %collective-permute-start.10 = (bf16[4,32,128]{2,1,0:T(8,128)(2,1)S(1)}, bf16[4,32,128]{2,1,0:T(8,128)(2,1)S(1)}, u32[]{:S(2)}, u32[]{:S(2)}) collective-permute-start(bf16[4,32,128]{2,1,0:T(8,128)(2,1)S(1)} %merge.1.refs_0_), channel_id=1, source_target_pairs={{0,8},{4,12},{8,0},{12,4},{1,9},{5,13},{9,1},{13,5},{2,10},{6,14},... | collective-permute-start | bytes 98312 | tf_op jit(solution)/shard_map/ppermute | solution.py:36
  25.8 9.2 %collective-permute-start.9 = (bf16[4,32,128]{2,1,0:T(8,128)(2,1)S(1)}, bf16[4,32,128]{2,1,0:T(8,128)(2,1)S(1)}, u32[]{:S(2)}, u32[]{:S(2)}) collective-permute-start(bf16[4,32,128]{2,1,0:T(8,128)(2,1)S(1)} %merge.1.refs_0_), channel_id=1, source_target_pairs={{0,4},{4,0},{8,12},{12,8},{1,5},{5,1},{9,13},{13,9},{2,6},{6,2},{1... | collective-permute-start | bytes 98312 | tf_op jit(solution)/shard_map/ppermute | solution.py:36
  38.7 3.1 %collective-permute-start.14 = (f32[4,1024]{1,0:T(4,128)S(1)}, f32[4,1024]{1,0:T(4,128)S(1)}, u32[]{:S(2)}, u32[]{:S(2)}) collective-permute-start(f32[4,1024]{1,0:T(4,128)S(1)} %shard_map.87), channel_id=1, source_target_pairs={{0,1},{1,0},{2,3},{3,2},{4,5},{5,4},{6,7},{7,6},{8,9},{9,8},{10,11... | collective-permute-start | bytes 49160 | tf_op jit(solution)/shard_map/ppermute | solution.py:36
  38.7 3.8 %collective-permute-start.12 = (f32[4,1024]{1,0:T(4,128)S(1)}, f32[4,1024]{1,0:T(4,128)S(1)}, u32[]{:S(2)}, u32[]{:S(2)}) collective-permute-start(f32[4,1024]{1,0:T(4,128)S(1)} %get-tuple-element.29), channel_id=1, source_target_pairs={{0,2},{1,3},{2,0},{3,1},{4,6},{5,7},{6,4},{7,5},{8,10},{9,11},{10,... | collective-permute-start | bytes 49160 | tf_op jit(solution)/shard_map/ppermute | solution.py:36
  39.7 3.2 %collective-permute-start.13 = (f32[4,1024]{1,0:T(4,128)S(1)}, f32[4,1024]{1,0:T(4,128)S(1)}, u32[]{:S(2)}, u32[]{:S(2)}) collective-permute-start(f32[4,1024]{1,0:T(4,128)S(1)} %get-tuple-element.30), channel_id=1, source_target_pairs={{0,3},{1,2},{2,1},{3,0},{4,7},{5,6},{6,5},{7,4},{8,11},{9,10},{10,... | collective-permute-start | bytes 49160 | tf_op jit(solution)/shard_map/ppermute | solution.py:36
